TPU v7x, 256 devices: a whole 4x4x8 slice. The times are simulated.
256 devices in a mesh: row: 32 (over y_lo, z, core), col: 8 (over y_hi, x).
Axes of the slice: x: 4, y: 4 (y_hi: 2, y_lo: 2; y = y_hi * 2 + y_lo), z: 8, core: 2. Of those that a mesh axis runs over, the one named last changes fastest.
Arguments:
- features: bfloat16 [262144, 256], P(('row', 'col')), may hold values from -6 to 6
- tile_values: bfloat16 [32, 8, 256, 128, 128], P('row', 'col'), may hold values from -0.09375 to 0.09375
- tile_rows: int32 [32, 8, 256], P('row', 'col'), may hold values from 0 to 63
- tile_cols: int32 [32, 8, 256], P('row', 'col'), may hold values from 0 to 255
- tile_count: int32 [32, 8], P('row', 'col'), may hold values from 64 to 256, as said below
- weight: bfloat16 [256, 256], replicated, may hold values from -0.375 to 0.375
Outputs:
- layer_out: bfloat16 [262144, 256], P(('row', 'col'))
Inputs may be any that keep to these rules, and one draw needn't show every extreme that they name: `tile_count`: live slots of one row block and column group; some block is full in every draw.
All inputs are finite; a program needn't handle non-finite values.
Results may differ from a plain program's by a relative error of at most 0.015.
Values may be sent and summed in bfloat16 or wider, within the bound.
A program may use at most 128 MiB of HBM per device.

v0:
```python
import math

import jax
import jax.numpy as jnp
from jax import lax
from jax.sharding import PartitionSpec as P


def local(features, tile_values, tile_rows, tile_cols, tile_count, weight):
    slab_rows, width = features.shape
    tiles = tile_values.shape[2]
    side = tile_values.shape[3]
    values = tile_values.reshape(tiles, side, side)
    rows_idx = tile_rows.reshape(tiles)
    cols_idx = tile_cols.reshape(tiles)
    count = tile_count.reshape(())
    group = lax.all_gather(features, "row", axis=0, tiled=True)
    col_count = group.shape[0] // side
    col_tiles = group.reshape(col_count, side, width)
    n_cols = lax.axis_size("col")
    row_tiles = n_cols * slab_rows // side
    block_len = math.gcd(tiles, 64)

    def accumulate(turn, carry):
        start = turn * block_len
        vals = lax.dynamic_slice_in_dim(values, start, block_len, 0)
        picks = lax.dynamic_slice_in_dim(cols_idx, start, block_len, 0)
        targets = lax.dynamic_slice_in_dim(rows_idx, start, block_len, 0)
        inputs = jnp.take(col_tiles, picks, axis=0)
        products = jnp.einsum("kij,kjf->kif", vals, inputs, preferred_element_type=jnp.float32)
        live = (start + jnp.arange(block_len, dtype=jnp.int32) < count).astype(jnp.float32)
        products = products * live[:, None, None]
        return carry.at[targets].add(products)

    carry = lax.fori_loop(
        0, tiles // block_len, accumulate, jnp.zeros((row_tiles, side, width), jnp.float32)
    )
    rounded = lax.optimization_barrier(carry.reshape(row_tiles * side, width).astype(jnp.bfloat16))
    partial_value = rounded.astype(jnp.float32)
    total = lax.psum(partial_value.astype(jnp.bfloat16), "col").astype(jnp.float32)
    summed = lax.dynamic_slice_in_dim(total, lax.axis_index("col") * slab_rows, slab_rows, 0)
    aggregated = summed.astype(jnp.bfloat16)
    return jnp.dot(aggregated, weight, preferred_element_type=jnp.float32).astype(jnp.bfloat16)


def solution(mesh):
    return jax.shard_map(
        local,
        mesh=mesh,
        in_specs=(
            P(("row", "col"), None),
            P("row", "col", None, None, None),
            P("row", "col", None),
            P("row", "col", None),
            P("row", "col"),
            P(),
        ),
        out_specs=P(("row", "col"), None),
        check_vma=False,
    )
```

profile of v0, /device:TPU:1, one launch (start us, length us, event | category | flops | bytes accessed | tf_op | source)
XLA Modules:
  0.0 392.5 jit_solution(11642625156492963269)
XLA Ops:
  6.5 0.0 copy-start
  6.5 0.0 all-gather.2.cloned.1.call-start
  6.5 0.7 all-gather.2.cloned.1.call-update
  7.3 0.0 all-reduce.2.cloned.1.call-start
  7.3 105.8 %all-gather.2.cloned.1.call-done = bf16[32768,256]{1,0:T(8,128)(2,1)} async-done(((bf16[1024,256]{1,0:T(8,128)(2,1)}), bf16[32768,256]{1,0:T(8,128)(2,1)}) %all-gather.2.cloned.1.call-update) | async-done | bytes 16777232 | tf_op jit(solution)/shard_map/all_gather | solution.py:17
  113.1 4.2 %broadcast_in_dim.37 = f32[64,128,256]{2,1,0:T(8,128)} broadcast(f32[]{:T(128)} %constant.62.clone.1), dimensions={} | broadcast | bytes 8388612 | tf_op jit(solution)/shard_map/broadcast_in_dim | solution.py:36
  117.3 0.0 copy-done.2
  117.4 145.0 %while.13 = (s32[]{:T(128)}, f32[64,128,256]{2,1,0:T(8,128)}, s32[256]{0:T(256)S(1)}, bf16[256,128,128]{2,1,0:T(8,128)(2,1)}, s32[256]{0:T(256)S(1)}, /*index=5*...) while((s32[]{:T(128)}, f32[64,128,256]{2,1,0:T(8,128)}, ...), condition=%wide.region_2.3_spmd, body=%wide.region_0.2_spmd.sunk | while | flops 543164160 | bytes 48241208 | solution.py:35
  117.4 0.1 compare_select_fusion.4
  117.4 0.7 compare_and_fusion.2
  118.2 8.6 %gather_fusion = bf16[64,128,256]{2,1,0:T(8,128)(2,1)} fusion(bf16[256,128,256]{2,1,0:T(8,128)(2,1)} %get-tuple-element.223, s32[1024]{0:T(1024)S(1)} %pad_clamp_fusion.2), kind=kCustom, calls=%fused_computation.clone.1 | custom fusion | bytes 8388864 | tf_op jit(solution)/shard_map/while/body/eval_jaxpr/jit(_take)/gather | solution.py:29
  126.8 7.4 %broadcast_multiply_fusion.2 = f32[64,128,256]{2,1,0:T(8,128)} fusion(f32[64]{0:T(128)S(1)} %get-tuple-element.193, bf16[64,128,256]{2,1,0:T(8,128)(2,1)} %gather_fusion, pred[64]{0:T(512)(128)(4,1)S(1)} %get-tuple-element.195, bf16[256,128,128]{2,1,0:T(8,128)(2,1)} %get-tuple-element.221, s32[]{:T(128)S(6)} %select_n.49), kind=kOutput, calls=%fused_computation.2.clone.1 | convolution fusion | flops 541065216 | bytes 14680388 | tf_op jit(solution)/shard_map/while/body/eval_jaxpr/kij,kjf->kif/dot_general | solution.py:30
  134.2 19.3 %scatter_fusion = f32[64,128,256]{2,1,0:T(8,128)} fusion(f32[64,128,256]{2,1,0:T(8,128)} %get-tuple-element.208, s32[64]{0:T(128)S(1)} %compare_select_fusion.4, f32[64,128,256]{2,1,0:T(8,128)} %broadcast_multiply_fusion.2), kind=kCustom, calls=%fused_computation.1.clone.1 | custom fusion | flops 2097152 | bytes 25166080 | tf_op jit(solution)/shard_map/while/body/eval_jaxpr/scatter-add | solution.py:33
  153.4 0.1 compare_select_fusion.4
  153.5 0.7 compare_and_fusion.2
  154.3 8.6 %gather_fusion = bf16[64,128,256]{2,1,0:T(8,128)(2,1)} fusion(bf16[256,128,256]{2,1,0:T(8,128)(2,1)} %get-tuple-element.223, s32[1024]{0:T(1024)S(1)} %pad_clamp_fusion.2), kind=kCustom, calls=%fused_computation.clone.1 | custom fusion | bytes 8388864 | tf_op jit(solution)/shard_map/while/body/eval_jaxpr/jit(_take)/gather | solution.py:29
  162.9 7.4 %broadcast_multiply_fusion.2 = f32[64,128,256]{2,1,0:T(8,128)} fusion(f32[64]{0:T(128)S(1)} %get-tuple-element.193, bf16[64,128,256]{2,1,0:T(8,128)(2,1)} %gather_fusion, pred[64]{0:T(512)(128)(4,1)S(1)} %get-tuple-element.195, bf16[256,128,128]{2,1,0:T(8,128)(2,1)} %get-tuple-element.221, s32[]{:T(128)S(6)} %select_n.49), kind=kOutput, calls=%fused_computation.2.clone.1 | convolution fusion | flops 541065216 | bytes 14680388 | tf_op jit(solution)/shard_map/while/body/eval_jaxpr/kij,kjf->kif/dot_general | solution.py:30
  170.3 19.7 %scatter_fusion = f32[64,128,256]{2,1,0:T(8,128)} fusion(f32[64,128,256]{2,1,0:T(8,128)} %get-tuple-element.208, s32[64]{0:T(128)S(1)} %compare_select_fusion.4, f32[64,128,256]{2,1,0:T(8,128)} %broadcast_multiply_fusion.2), kind=kCustom, calls=%fused_computation.1.clone.1 | custom fusion | flops 2097152 | bytes 25166080 | tf_op jit(solution)/shard_map/while/body/eval_jaxpr/scatter-add | solution.py:33
  189.9 0.1 compare_select_fusion.4
  190.0 0.7 compare_and_fusion.2
  190.7 8.6 %gather_fusion = bf16[64,128,256]{2,1,0:T(8,128)(2,1)} fusion(bf16[256,128,256]{2,1,0:T(8,128)(2,1)} %get-tuple-element.223, s32[1024]{0:T(1024)S(1)} %pad_clamp_fusion.2), kind=kCustom, calls=%fused_computation.clone.1 | custom fusion | bytes 8388864 | tf_op jit(solution)/shard_map/while/body/eval_jaxpr/jit(_take)/gather | solution.py:29
  199.4 7.4 %broadcast_multiply_fusion.2 = f32[64,128,256]{2,1,0:T(8,128)} fusion(f32[64]{0:T(128)S(1)} %get-tuple-element.193, bf16[64,128,256]{2,1,0:T(8,128)(2,1)} %gather_fusion, pred[64]{0:T(512)(128)(4,1)S(1)} %get-tuple-element.195, bf16[256,128,128]{2,1,0:T(8,128)(2,1)} %get-tuple-element.221, s32[]{:T(128)S(6)} %select_n.49), kind=kOutput, calls=%fused_computation.2.clone.1 | convolution fusion | flops 541065216 | bytes 14680388 | tf_op jit(solution)/shard_map/while/body/eval_jaxpr/kij,kjf->kif/dot_general | solution.py:30
  206.7 19.3 %scatter_fusion = f32[64,128,256]{2,1,0:T(8,128)} fusion(f32[64,128,256]{2,1,0:T(8,128)} %get-tuple-element.208, s32[64]{0:T(128)S(1)} %compare_select_fusion.4, f32[64,128,256]{2,1,0:T(8,128)} %broadcast_multiply_fusion.2), kind=kCustom, calls=%fused_computation.1.clone.1 | custom fusion | flops 2097152 | bytes 25166080 | tf_op jit(solution)/shard_map/while/body/eval_jaxpr/scatter-add | solution.py:33
  226.0 0.1 compare_select_fusion.4
  226.1 0.7 compare_and_fusion.2
  226.8 8.6 %gather_fusion = bf16[64,128,256]{2,1,0:T(8,128)(2,1)} fusion(bf16[256,128,256]{2,1,0:T(8,128)(2,1)} %get-tuple-element.223, s32[1024]{0:T(1024)S(1)} %pad_clamp_fusion.2), kind=kCustom, calls=%fused_computation.clone.1 | custom fusion | bytes 8388864 | tf_op jit(solution)/shard_map/while/body/eval_jaxpr/jit(_take)/gather | solution.py:29
  235.5 7.4 %broadcast_multiply_fusion.2 = f32[64,128,256]{2,1,0:T(8,128)} fusion(f32[64]{0:T(128)S(1)} %get-tuple-element.193, bf16[64,128,256]{2,1,0:T(8,128)(2,1)} %gather_fusion, pred[64]{0:T(512)(128)(4,1)S(1)} %get-tuple-element.195, bf16[256,128,128]{2,1,0:T(8,128)(2,1)} %get-tuple-element.221, s32[]{:T(128)S(6)} %select_n.49), kind=kOutput, calls=%fused_computation.2.clone.1 | convolution fusion | flops 541065216 | bytes 14680388 | tf_op jit(solution)/shard_map/while/body/eval_jaxpr/kij,kjf->kif/dot_general | solution.py:30
  242.8 19.5 %scatter_fusion = f32[64,128,256]{2,1,0:T(8,128)} fusion(f32[64,128,256]{2,1,0:T(8,128)} %get-tuple-element.208, s32[64]{0:T(128)S(1)} %compare_select_fusion.4, f32[64,128,256]{2,1,0:T(8,128)} %broadcast_multiply_fusion.2), kind=kCustom, calls=%fused_computation.1.clone.1 | custom fusion | flops 2097152 | bytes 25166080 | tf_op jit(solution)/shard_map/while/body/eval_jaxpr/scatter-add | solution.py:33
  262.3 5.9 %convert_element_type.28 = bf16[64,128,256]{2,1,0:T(8,128)(2,1)} convert(f32[64,128,256]{2,1,0:T(8,128)} %get-tuple-element.129) | non-fusion elementwise | flops 2097152 | bytes 12582912 | tf_op jit(solution)/shard_map/convert_element_type | solution.py:38
  268.3 0.0 all-reduce.2.cloned.1.call-update
  268.3 115.2 %all-reduce.2.cloned.1.call-done = bf16[8192,256]{1,0:T(8,128)(2,1)} async-done(((bf16[8192,256]{1,0:T(8,128)(2,1)}), bf16[8192,256]{1,0:T(8,128)(2,1)}) %all-reduce.2.cloned.1.call-update) | async-done | bytes 4194320 | tf_op jit(solution)/shard_map/psum | solution.py:40
  383.5 2.1 convolution_convert_fusion
  (8 shorter events, 0.0 us)
Async XLA Ops:
  6.5 377.0 %copy-start = (bf16[256,256]{1,0:T(8,128)(2,1)S(1)}, bf16[256,256]{1,0:T(8,128)(2,1)}, u32[]{:S(2)}) copy-start(bf16[256,256]{1,0:T(8,128)(2,1)} %param.13) | copy-start | bytes 393220
  6.5 110.8 %copy-start.2 = (s32[1,1,256]{2,1,0:T(1,128)S(1)}, s32[1,1,256]{2,1,0:T(1,128)}, u32[]{:S(2)}) copy-start(s32[1,1,256]{2,1,0:T(1,128)} %param.10) | copy-start | bytes 3076
  6.5 110.8 %copy-start.1 = (s32[1,1,256]{2,1,0:T(1,128)S(1)}, s32[1,1,256]{2,1,0:T(1,128)}, u32[]{:S(2)}) copy-start(s32[1,1,256]{2,1,0:T(1,128)} %param.11) | copy-start | bytes 3076
  6.5 106.6 %all-gather.2.cloned.1.call-start = ((), (), s32[]{:S(2)}) async-start(), calls=%async_computation | async-start | bytes 17301504 | tf_op jit(solution)/shard_map/all_gather | solution.py:17
  7.3 376.2 %all-reduce.2.cloned.1.call-start = ((), (), s32[]{:S(2)}) async-start(), calls=%async_computation.1 | async-start | bytes 8388608 | tf_op jit(solution)/shard_map/psum | solution.py:40
Sparse Core Ops, SparseCore 0:
  9.2 103.8 all-gather.1
  268.4 115.0 all-reduce.1
where the time goes:
time: 393 us; the launch traced here: 392 us
  waiting for transfers between devices  222 us (56%)
  other arithmetic  86.8 us (22%)
  local copies, waits for them, and re-layouts  38.8 us (10%)
  matrix products  31.6 us (8%)
  between operations  13.4 us (3%)
    psum x1, waiting for transfers between devices, local(): lax.psum(partial_value.astype(jnp.bfloat16), 'col').astype(jnp.float32)  115 us
    all_gather x1, waiting for transfers between devices, local(): group = lax.all_gather(features, 'row', axis=0, tiled=True)  106 us
    scatter-add x4, other arithmetic, accumulate(): return carry.at[targets].add(products)  77.7 us
    gather x4, local copies, waits for them, and re-layouts, accumulate(): inputs = jnp.take(col_tiles, picks, axis=0)  34.5 us
    dot_general x4, matrix products, accumulate(): jnp.einsum('kij,kjf->kif', vals, inputs, preferred_element_type=jnp.float32)  29.5 us
  transfers between devices with their start and end apart: 2, of which 2 were waited for; matrix products, arithmetic and copies ran while one was open for 0% of the time, Pallas kernels for 0%

commit v1 on v0

v1 whole, which is shorter than its diff:
```python
import jax
import jax.numpy as jnp
from jax import lax
from jax.experimental import pallas as pl
from jax.experimental.pallas import tpu as pltpu
from jax.sharding import PartitionSpec as P

UNROLL = 4
DEPTH = 4


def tile_sums(rows, cols, count, a_hbm, x_hbm, out, acc, a_buf, x_buf, a_sem, x_sem):
    row_tiles = out.shape[0]
    n = count[0]
    groups = (n + UNROLL - 1) // UNROLL

    def copies(g, slot):
        start = pl.multiple_of(g * UNROLL, UNROLL)
        yield pltpu.make_async_copy(a_hbm.at[pl.ds(start, UNROLL)], a_buf.at[slot], a_sem.at[slot])
        for j in range(UNROLL):
            yield pltpu.make_async_copy(x_hbm.at[cols[start + j]], x_buf.at[slot, j], x_sem.at[slot, j])

    def fetch(g, slot):
        for copy in copies(g, slot):
            copy.start()

    for d in range(DEPTH - 1):
        @pl.when(d < groups)
        def _():
            fetch(d, d)

    @pl.loop(0, row_tiles)
    def _(i):
        acc[i] = jnp.zeros(acc.shape[1:], acc.dtype)

    @pl.loop(0, groups)
    def _(g):
        slot = lax.rem(g, DEPTH)
        for copy in copies(g, slot):
            copy.wait()

        @pl.when(g + DEPTH - 1 < groups)
        def _():
            fetch(g + DEPTH - 1, lax.rem(g + DEPTH - 1, DEPTH))

        for j in range(UNROLL):
            k = g * UNROLL + j
            row = jnp.where(k < n, rows[k], row_tiles)
            acc[row] += jnp.dot(a_buf[slot, j], x_buf[slot, j], preferred_element_type=jnp.float32)

    @pl.loop(0, row_tiles)
    def _(i):
        out[i] = acc[i].astype(out.dtype)


def local_sums(rows, cols, count, values, group, row_tiles):
    side, width = group.shape[1:]
    smem = pl.BlockSpec(memory_space=pltpu.SMEM)
    hbm = pl.BlockSpec(memory_space=pl.ANY)
    return pl.pallas_call(
        tile_sums,
        out_shape=jax.ShapeDtypeStruct((row_tiles, side, width), jnp.bfloat16),
        in_specs=[smem, smem, smem, hbm, hbm],
        out_specs=pl.BlockSpec(memory_space=pltpu.VMEM),
        scratch_shapes=[
            pltpu.VMEM((row_tiles + 1, side, width), jnp.float32),
            pltpu.VMEM((DEPTH, UNROLL, side, side), jnp.bfloat16),
            pltpu.VMEM((DEPTH, UNROLL, side, width), jnp.bfloat16),
            pltpu.SemaphoreType.DMA((DEPTH,)),
            pltpu.SemaphoreType.DMA((DEPTH, UNROLL)),
        ],
        name="tile_sums",
    )(rows, cols, count, values, group)


def local(features, tile_values, tile_rows, tile_cols, tile_count, weight):
    slab_rows, width = features.shape
    tiles, side = tile_values.shape[2:4]
    values = tile_values.reshape(tiles, side, side)
    row_tiles = lax.axis_size("col") * slab_rows // side
    group = lax.all_gather(features, "row", axis=0, tiled=True).reshape(-1, side, width)
    partial = local_sums(
        tile_rows.reshape(tiles), tile_cols.reshape(tiles), tile_count.reshape(1), values, group, row_tiles
    )
    summed = lax.psum_scatter(partial.reshape(row_tiles * side, width), "col", scatter_dimension=0, tiled=True)
    return jnp.dot(summed, weight, preferred_element_type=jnp.float32).astype(jnp.bfloat16)


def solution(mesh):
    return jax.shard_map(
        local,
        mesh=mesh,
        in_specs=(
            P(("row", "col"), None),
            P("row", "col", None, None, None),
            P("row", "col", None),
            P("row", "col", None),
            P("row", "col"),
            P(),
        ),
        out_specs=P(("row", "col"), None),
        check_vma=False,
    )
```

time: 393 us -> 237 us (0.60)
  other arithmetic: 86.8 us -> 0 us
  local copies, waits for them, and re-layouts: 38.8 us -> 0.01 us
  matrix products: 31.6 us -> 2.13 us
  waiting for transfers between devices: 222 us -> 203 us
  Pallas kernels: 0 us -> 16.5 us
    psum x1 -> x0, waiting for transfers between devices: 115 us -> none  [local(): lax.psum(partial_value.astype(jnp.bfloat16), 'col').astype(jnp.float32)]
    reduce_scatter x0 -> x1, waiting for transfers between devices: none -> 97.5 us  [local(): lax.psum_scatter(partial.reshape(row_tiles * side, width), 'col', scatter...]
    scatter-add x4 -> x0, other arithmetic: 77.7 us -> none  [accumulate(): return carry.at[targets].add(products)]
    gather x4 -> x0, local copies, waits for them, and re-layouts: 34.5 us -> none  [accumulate(): inputs = jnp.take(col_tiles, picks, axis=0)]
    dot_general x5 -> x1, matrix products: 31.6 us -> 2.13 us  [local(): jnp.dot(summed, weight, preferred_element_type=jnp.float32)]
    pallas_call x0 -> x1, Pallas kernels: none -> 16.5 us  [local_sums(): pl.pallas_call(tile_sums, out_shape=jax.ShapeDtypeStruct((row_tiles, side...]
    convert_element_type x1 -> x0, other arithmetic: 5.93 us -> none  [local(): carry.reshape(row_tiles * side, width).astype(jnp.bfloat16)]
    broadcast_in_dim x1 -> x0, local copies, waits for them, and re-layouts: 4.24 us -> none  [local(): jnp.zeros((row_tiles, side, width), jnp.float32)]
where the time goes in v1:
time: 237 us; the launch traced here: 236 us
  waiting for transfers between devices  203 us (86%)
  Pallas kernels  16.5 us (7%)
  between operations  14.1 us (6%)
    all_gather x1, waiting for transfers between devices, local(): lax.all_gather(features, 'row', axis=0, tiled=True).reshape(-1, side, width)  105 us
    reduce_scatter x1, waiting for transfers between devices, local(): lax.psum_scatter(partial.reshape(row_tiles * side, width), 'col', scatter...  97.5 us
    pallas_call x1, Pallas kernels, local_sums(): pl.pallas_call(tile_sums, out_shape=jax.ShapeDtypeStruct((row_tiles, side...  16.5 us
  transfers between devices with their start and end apart: 2, of which 2 were waited for; matrix products, arithmetic and copies ran while one was open for 0% of the time, Pallas kernels for 0%

profile of v1, /device:TPU:1, one launch (start us, length us, event | category | flops | bytes accessed | tf_op | source)
XLA Modules:
  0.0 236.1 jit_solution(9823573302137135538)
XLA Ops:
  6.5 0.0 copy-start
  6.5 0.0 all-gather.2.cloned.1.call-start
  6.5 0.7 all-gather.2.cloned.1.call-update
  7.3 0.0 reduce-scatter.2.cloned.1.call-start
  8.0 105.2 %all-gather.2.cloned.1.call-done = bf16[32768,256]{1,0:T(8,128)(2,1)} async-done(((bf16[1024,256]{1,0:T(8,128)(2,1)}), bf16[32768,256]{1,0:T(8,128)(2,1)}) %all-gather.2.cloned.1.call-update) | async-done | bytes 16777232 | tf_op jit(solution)/shard_map/all_gather | solution.py:81
  113.1 16.5 %tile_sums.1 = bf16[64,128,256]{2,1,0:T(8,128)(2,1)} custom-call(s32[256]{0:T(256)} %bitcast.12, s32[256]{0:T(256)} %bitcast.13, s32[1]{0:T(128)} %bitcast.8.count, bf16[256,128,128]{2,1,0:T(8,128)(2,1)} %bitcast.11, bf16[256,128,256]{2,1,0:T(8,128)(2,1)} %bitcast.9), custom_call_target="tpu_custom_call" | custom-call | tf_op jit(solution)/shard_map/tile_sums/pallas_call | solution.py:60
  129.6 0.0 reduce-scatter.2.cloned.1.call-update
  129.6 97.5 %reduce-scatter.2.cloned.1.call-done = bf16[1024,256]{1,0:T(8,128)(2,1)} async-done(((bf16[8192,256]{1,0:T(8,128)(2,1)}), bf16[1024,256]{1,0:T(8,128)(2,1)}) %reduce-scatter.2.cloned.1.call-update) | async-done | bytes 524304 | tf_op jit(solution)/shard_map/reduce_scatter | solution.py:85
  227.1 0.0 copy-done
  227.1 2.1 convolution_convert_fusion
Async XLA Ops:
  6.5 220.6 %copy-start = (bf16[256,256]{1,0:T(8,128)(2,1)S(1)}, bf16[256,256]{1,0:T(8,128)(2,1)}, u32[]{:S(2)}) copy-start(bf16[256,256]{1,0:T(8,128)(2,1)} %param.11) | copy-start | bytes 393220
  6.5 106.6 %all-gather.2.cloned.1.call-start = ((), (), s32[]{:S(2)}) async-start(), calls=%async_computation.1 | async-start | bytes 17301504 | tf_op jit(solution)/shard_map/all_gather | solution.py:81
  7.3 219.9 %reduce-scatter.2.cloned.1.call-start = ((), (), s32[]{:S(2)}) async-start(), calls=%async_computation.2 | async-start | bytes 4718592 | tf_op jit(solution)/shard_map/reduce_scatter | solution.py:85
Sparse Core Ops, SparseCore 0:
  9.2 103.8 all-gather.1
  129.7 97.3 reduce-scatter.1

commit v2 on v1

--- a/solution.py
+++ b/solution.py
@@ -4,6 +4,280 @@
 from jax.experimental import pallas as pl
 from jax.experimental.pallas import tpu as pltpu
 from jax.sharding import PartitionSpec as P
+
+MESH = pl.DeviceIdType.MESH
+SLAB = 8
+RING = 8
+
+
+def enter(devices):
+    barrier = pltpu.get_barrier_semaphore()
+    for device in devices:
+        pl.semaphore_signal(barrier, inc=1, device_id=device, device_id_type=MESH)
+    pl.semaphore_wait(barrier, len(devices))
+
+
+class Messages:
+    def __init__(self, send_sem, recv_sem):
+        self.send_sem, self.recv_sem = send_sem, recv_sem
+        self.index, self.sent = {}, []
+
+    def slot(self, key):
+        return self.index.setdefault(key, len(self.index))
+
+    def copy(self, key, src, dst, device):
+        slot = self.slot(key)
+        return pltpu.make_async_remote_copy(
+            src_ref=src, dst_ref=dst, send_sem=self.send_sem.at[slot], recv_sem=self.recv_sem.at[slot],
+            device_id=device, device_id_type=MESH,
+        )
+
+    def send(self, key, src, dst, device):
+        copy = self.copy(key, src, dst, device)
+        copy.start()
+        self.sent.append(copy)
+
+    def arrive(self, key, dst, device):
+        self.copy(key, dst, dst, device).wait_recv()
+
+    def drain(self):
+        for copy in self.sent:
+            copy.wait_send()
+
+
+GATHER_MESSAGES = 91
+
+
+def gather_kernel(own_ref, group, send_sem, recv_sem, local_sem):
+    row = lax.axis_index("row")
+    half, z, core = row // 16, lax.rem(row // 2, RING), lax.rem(row, 2)
+
+    def position(h, depth, c):
+        return h * 16 + lax.rem(depth + 2 * RING, RING) * 2 + c
+
+    up = {"row": position(half, z + 1, core)}
+    down = {"row": position(half, z - 1, core)}
+    side = {"row": position(1 - half, z, core)}
+    twin = {"row": position(half, z, 1 - core)}
+    enter((up, down, side, twin))
+    messages = Messages(send_sem, recv_sem)
+
+    def at(h, depth, c, start, size):
+        return group.at[pl.ds(position(h, depth, c) * SLAB + start, size)]
+
+    keep = pltpu.make_async_copy(own_ref, at(half, z, core, 0, SLAB), local_sem)
+    keep.start()
+    low, high = (0, 4), (4, 4)
+    shared, shared_low, shared_high = (2, 4), (2, 2), (4, 2)
+    rest_low, rest_high = (0, 2), (6, 2)
+
+    def from_own(piece):
+        return own_ref.at[pl.ds(piece[0], piece[1])]
+
+    def ring_send(way, step, mine, piece):
+        origin = z - way * (step - 1)
+        owner = half if mine else 1 - half
+        dst = at(owner, origin, core, *piece)
+        src = from_own(piece) if mine and step == 1 else dst
+        messages.send(("ring", way, step, mine, piece), src, dst, up if way > 0 else down)
+
+    def twin_send(key, src, dst):
+        messages.send(("twin",) + key, src, dst, twin)
+
+    waiting_twin = []
+
+    def ring_arrive(way, step, mine, piece, last):
+        origin = z - way * step
+        owner = half if mine else 1 - half
+        here = at(owner, origin, core, *piece)
+        key = ("ring", way, step, mine, piece)
+        messages.arrive(key, here, up)
+        if step < last:
+            ring_send(way, step + 1, mine, piece)
+        if mine:
+            rest = rest_low if piece == low else rest_high
+            part = at(half, origin, core, *rest)
+            messages.send(("side", way, step, rest), part, part, side)
+        twin_send(key, here, here)
+        waiting_twin.append((key, at(owner, origin, 1 - core, *piece)))
+
+    def side_arrive(key, origin, piece):
+        here = at(1 - half, origin, core, *piece)
+        messages.arrive(key, here, side)
+        twin_send(key, here, here)
+        waiting_twin.append((key, at(1 - half, origin, 1 - core, *piece)))
+
+    ring_send(1, 1, True, low)
+    ring_send(-1, 1, True, high)
+    messages.send(("side", 0, 0, shared), from_own(shared), at(half, z, core, *shared), side)
+    ring_send(1, 1, True, high)
+    ring_send(-1, 1, True, low)
+    for piece in (rest_low, rest_high):
+        messages.send(("side", 0, 0, piece), from_own(piece), at(half, z, core, *piece), side)
+    twin_send(("own",), own_ref, at(half, z, core, 0, SLAB))
+    waiting_twin.append((("own",), at(half, z, 1 - core, 0, SLAB)))
+
+    for step in range(1, 5):
+        ring_arrive(1, step, True, low, 4)
+        ring_arrive(-1, step, True, high, 4)
+        if step == 1:
+            side_arrive(("side", 0, 0, shared), z, shared)
+            ring_send(1, 1, False, shared_low)
+            ring_send(-1, 1, False, shared_high)
+            ring_send(1, 1, False, shared_high)
+            ring_send(-1, 1, False, shared_low)
+        if step < 4:
+            ring_arrive(1, step, True, high, 3)
+            ring_arrive(-1, step, True, low, 3)
+        if step == 1:
+            side_arrive(("side", 0, 0, rest_low), z, rest_low)
+            side_arrive(("side", 0, 0, rest_high), z, rest_high)
+        ring_arrive(1, step, False, shared_low, 4)
+        ring_arrive(-1, step, False, shared_high, 4)
+        if step < 4:
+            ring_arrive(1, step, False, shared_high, 3)
+            ring_arrive(-1, step, False, shared_low, 3)
+        side_arrive(("side", 1, step, rest_low), z - step, rest_low)
+        side_arrive(("side", -1, step, rest_high), z + step, rest_high)
+        if step < 4:
+            side_arrive(("side", 1, step, rest_high), z - step, rest_high)
+            side_arrive(("side", -1, step, rest_low), z + step, rest_low)
+    for key, here in waiting_twin:
+        messages.arrive(("twin",) + key, here, twin)
+    keep.wait()
+    messages.drain()
+    assert len(messages.index) == GATHER_MESSAGES, len(messages.index)
+
+
+def gather_group(own):
+    n, side, width = own.shape
+    return pl.pallas_call(
+        gather_kernel,
+        out_shape=jax.ShapeDtypeStruct((4 * RING * n, side, width), own.dtype),
+        in_specs=[pl.BlockSpec(memory_space=pltpu.VMEM)],
+        out_specs=pl.BlockSpec(memory_space=pl.ANY),
+        scratch_shapes=[
+            pltpu.SemaphoreType.DMA((GATHER_MESSAGES,)),
+            pltpu.SemaphoreType.DMA((GATHER_MESSAGES,)),
+            pltpu.SemaphoreType.DMA,
+        ],
+        compiler_params=pltpu.CompilerParams(collective_id=0, has_side_effects=True),
+        name="gather_group",
+    )(own)
+
+
+SCATTER_MESSAGES = 20
+
+
+def scatter_kernel(part, out, x_in, turn, total, y_in, relay, send_sem, recv_sem):
+    row, col = lax.axis_index("row"), lax.axis_index("col")
+    y_lo, y_hi, x = row // 16, col // 4, lax.rem(col, 4)
+
+    def x_peer(way):
+        return {"col": y_hi * 4 + lax.rem(x + way + 4, 4)}
+
+    def y_peer(way):
+        y = lax.rem(y_hi * 2 + y_lo + way + 4, 4)
+        return {"row": lax.rem(row, 16) + lax.rem(y, 2) * 16, "col": (y // 2) * 4 + x}
+
+    peers = {("x", 1): x_peer(1), ("x", -1): x_peer(-1), ("y", 1): y_peer(1), ("y", -1): y_peer(-1)}
+    enter(tuple(peers.values()))
+    messages = Messages(send_sem, recv_sem)
+    both = (1, -1)
+
+    def chunk(far, way, start):
+        band = 1 - y_hi if far else y_hi
+        return pl.ds((band * 4 + lax.rem(x + way + 4, 4)) * SLAB + start, 4)
+
+    def x_send(kind, far, way, src):
+        messages.send(("x", kind, far, way), src, x_in.at[kind, far, (way + 1) // 2], peers["x", way])
+
+    def x_arrive(kind, far, way):
+        here = x_in.at[kind, far, (way + 1) // 2]
+        messages.arrive(("x", kind, far, way), here, peers["x", way])
+        return here
+
+    def through(way):
+        return 0 if way > 0 else 4
+
+    def first(far):
+        for way in both:
+            x_send(0, far, way, part.at[chunk(far, 2 * way, through(way))])
+        for way in both:
+            x_send(1, far, way, part.at[chunk(far, way, through(-way))])
+
+    def second(far):
+        for way in both:
+            here = x_arrive(0, far, way)
+            base = chunk(far, way, through(way)).start
+            for t in range(4):
+                turn[far, (way + 1) // 2, t] = (
+                    part[base + t].astype(jnp.float32) + here[t].astype(jnp.float32)
+                ).astype(turn.dtype)
+            x_send(2, far, way, turn.at[far, (way + 1) // 2])
+
+    def last(far, extra, store):
+        for way in both:
+            one = x_arrive(1, far, -way)
+            two = x_arrive(2, far, way)
+            more = extra(way)
+            base = chunk(far, 0, through(way)).start
+            for t in range(4):
+                value = part[base + t].astype(jnp.float32) + one[t].astype(jnp.float32) + two[t].astype(jnp.float32)
+                if more is not None:
+                    value = value + more[t].astype(jnp.float32)
+                store(way, t, value)
+            if far:
+                messages.send(("y", 0, way), total.at[(way + 1) // 2], relay.at[(way + 1) // 2], peers["y", way])
+
+    first(1)
+    second(1)
+    first(0)
+
+    def store_total(way, t, value):
+        total[(way + 1) // 2, t] = value.astype(total.dtype)
+
+    last(1, lambda way: None, store_total)
+    second(0)
+    for way in both:
+        here = relay.at[(way + 1) // 2]
+        messages.arrive(("y", 0, way), here, peers["y", way])
+        messages.send(("y", 1, way), here, y_in.at[(way + 1) // 2], peers["y", way])
+
+    def final(way):
+        here = y_in.at[(way + 1) // 2]
+        messages.arrive(("y", 1, way), here, peers["y", way])
+        return here
+
+    def store_out(way, t, value):
+        out[through(way) + t] = value.astype(out.dtype)
+
+    last(0, final, store_out)
+    messages.drain()
+
+
+def scatter_sums(part):
+    n, side, width = part.shape
+    piece = (4, side, width)
+    vmem = pl.BlockSpec(memory_space=pltpu.VMEM)
+    return pl.pallas_call(
+        scatter_kernel,
+        out_shape=jax.ShapeDtypeStruct((SLAB, side, width), part.dtype),
+        in_specs=[vmem],
+        out_specs=vmem,
+        scratch_shapes=[
+            pltpu.VMEM((3, 2, 2) + piece, part.dtype),
+            pltpu.VMEM((2, 2) + piece, part.dtype),
+            pltpu.VMEM((2,) + piece, part.dtype),
+            pltpu.VMEM((2,) + piece, part.dtype),
+            pltpu.VMEM((2,) + piece, part.dtype),
+            pltpu.SemaphoreType.DMA((SCATTER_MESSAGES,)),
+            pltpu.SemaphoreType.DMA((SCATTER_MESSAGES,)),
+        ],
+        compiler_params=pltpu.CompilerParams(collective_id=1, has_side_effects=True),
+        name="scatter_sums",
+    )(part)
+
 
 UNROLL = 4
 DEPTH = 4
@@ -78,11 +352,11 @@
     tiles, side = tile_values.shape[2:4]
     values = tile_values.reshape(tiles, side, side)
     row_tiles = lax.axis_size("col") * slab_rows // side
-    group = lax.all_gather(features, "row", axis=0, tiled=True).reshape(-1, side, width)
+    group = gather_group(features.reshape(slab_rows // side, side, width))
     partial = local_sums(
         tile_rows.reshape(tiles), tile_cols.reshape(tiles), tile_count.reshape(1), values, group, row_tiles
     )
-    summed = lax.psum_scatter(partial.reshape(row_tiles * side, width), "col", scatter_dimension=0, tiled=True)
+    summed = scatter_sums(partial).reshape(slab_rows, width)
     return jnp.dot(summed, weight, preferred_element_type=jnp.float32).astype(jnp.bfloat16)
 
 

time: 237 us -> 145 us (0.61)
  waiting for transfers between devices: 203 us -> 0 us
  Pallas kernels: 16.5 us -> 140 us
  between operations: 14.1 us -> 0.72 us
    pallas_call x0 -> x2, Pallas kernels: none -> 125 us  [the longest x1 76.5 us: gather_group(): pl.pallas_call(gather_kernel, out_shape=jax.ShapeDtypeStruct((4 * RING *...]
    all_gather x1 -> x0, waiting for transfers between devices: 105 us -> none  [local(): lax.all_gather(features, 'row', axis=0, tiled=True).reshape(-1, side, width)]
    reduce_scatter x1 -> x0, waiting for transfers between devices: 97.5 us -> none  [local(): lax.psum_scatter(partial.reshape(row_tiles * side, width), 'col', scatter...]
  transfers between devices with their start and end apart: 2 -> 0, of which waited for: 2 -> 0; matrix products, arithmetic and copies ran while one was open for 0% -> 0% of each run, Pallas kernels for 0% -> 0%
where the time goes in v2:
time: 145 us; the launch traced here: 142 us
  Pallas kernels  140 us (97%)
  matrix products  2.14 us (1%)
    pallas_call x1, Pallas kernels, gather_group(): pl.pallas_call(gather_kernel, out_shape=jax.ShapeDtypeStruct((4 * RING *...  76.5 us
    pallas_call x1, Pallas kernels, scatter_sums(): pl.pallas_call(scatter_kernel, out_shape=jax.ShapeDtypeStruct((SLAB, side...  48.2 us
    pallas_call x1, Pallas kernels, local_sums(): pl.pallas_call(tile_sums, out_shape=jax.ShapeDtypeStruct((row_tiles, side...  14.9 us

profile of v2, /device:TPU:1, one launch (start us, length us, event | category | flops | bytes accessed | tf_op | source)
XLA Modules:
  0.0 142.5 jit_solution(14510006265011208082)
XLA Ops:
  0.0 0.0 copy-start
  0.7 76.5 %gather_group.1.x_hbm = bf16[256,128,256]{2,1,0:T(8,128)(2,1)} custom-call(bf16[8,128,256]{2,1,0:T(8,128)(2,1)} %bitcast.11), custom_call_target="tpu_custom_call" | custom-call | tf_op jit(solution)/shard_map/gather_group/pallas_call | solution.py:154
  77.2 14.9 %tile_sums.1.part = bf16[64,128,256]{2,1,0:T(8,128)(2,1)} custom-call(s32[256]{0:T(256)} %bitcast.12, s32[256]{0:T(256)} %bitcast.13, s32[1]{0:T(128)} %bitcast.8.count, bf16[256,128,128]{2,1,0:T(8,128)(2,1)} %bitcast.9, bf16[256,128,256]{2,1,0:T(8,128)(2,1)} %gather_group.1.x_hbm), custom_call_target="tpu_custom_call" | custom-call | tf_op jit(solution)/shard_map/tile_sums/pallas_call | solution.py:334
  92.1 48.2 %scatter_sums.1 = bf16[8,128,256]{2,1,0:T(8,128)(2,1)} custom-call(bf16[64,128,256]{2,1,0:T(8,128)(2,1)} %tile_sums.1.part), custom_call_target="tpu_custom_call" | custom-call | tf_op jit(solution)/shard_map/scatter_sums/pallas_call | solution.py:263
  140.3 0.0 copy-done
  140.3 2.1 %convolution_convert_fusion = bf16[1024,256]{1,0:T(8,128)(2,1)} fusion(bf16[1024,256]{1,0:T(8,128)(2,1)} %bitcast.10, bf16[256,256]{1,0:T(8,128)(2,1)S(1)} %copy-done), kind=kOutput, calls=%fused_computation | convolution fusion | flops 134479872 | bytes 1179648 | tf_op jit(solution)/shard_map/dot_general | solution.py:360
Async XLA Ops:
  0.0 140.3 %copy-start = (bf16[256,256]{1,0:T(8,128)(2,1)S(1)}, bf16[256,256]{1,0:T(8,128)(2,1)}, u32[]{:S(2)}) copy-start(bf16[256,256]{1,0:T(8,128)(2,1)} %param.11) | copy-start | bytes 393220

commit v3 on v0

v3 whole, which is shorter than its diff:
```python
import jax
import jax.numpy as jnp
from jax import lax
from jax.experimental import pallas as pl
from jax.experimental.pallas import tpu as pltpu
from jax.sharding import PartitionSpec as P

MESH = pl.DeviceIdType.MESH
SLAB = 8
RING = 8
HALF = 128
STEPS = 8
PIECES = 8
GATHER_COPIES = 91
SCATTER_COPIES = 16
COPIES = GATHER_COPIES + SCATTER_COPIES


def plan_kernel(count, rows, cols, out):
    n = rows.shape[1]
    rows_in_all = 64
    f32 = jnp.float32
    lane = lax.broadcasted_iota(jnp.int32, (n, n), 1).astype(f32)
    sub = lax.broadcasted_iota(jnp.int32, (n, n), 0).astype(f32)
    spot = lax.broadcasted_iota(jnp.int32, (1, n), 1)
    row = jnp.where(spot < count[0], rows[...], rows_in_all).astype(f32)
    key = row * n + spot.astype(f32)

    def turned(line):
        return jnp.sum(jnp.where(lane == sub, line, 0.0), axis=1, keepdims=True)

    row_t, key_t, col_t = turned(row), turned(key), turned(cols[...].astype(f32))
    rank_t = jnp.sum(jnp.where(key < key_t, 1.0, 0.0), axis=1, keepdims=True)
    hit = rank_t == lane

    def placed(line):
        return jnp.sum(jnp.where(hit, line, 0.0), axis=0, keepdims=True)

    row_s = placed(row_t)
    keep = jnp.where((row_s == pltpu.roll(row_s, 1, 1)) & (spot > 0), 1.0, 0.0)
    upto = jnp.sum(jnp.where(row_t <= lane, 1.0, 0.0), axis=0, keepdims=True)
    below = jnp.sum(jnp.where(row_t < lane, 1.0, 0.0), axis=0, keepdims=True)
    lines = (placed(sub), placed(col_t), keep, jnp.maximum(upto - 1.0, 0.0), jnp.where(upto > below, 1.0, 0.0))
    for i, line in enumerate(lines):
        out[i : i + 1] = line.astype(jnp.int32)


def plan(count, rows, cols):
    vmem = pl.BlockSpec(memory_space=pltpu.VMEM)
    return pl.pallas_call(
        plan_kernel,
        out_shape=jax.ShapeDtypeStruct((8, rows.shape[1]), jnp.int32),
        in_specs=[pl.BlockSpec(memory_space=pltpu.SMEM), vmem, vmem],
        out_specs=vmem,
        name="plan",
    )(count, rows, cols)


def enter(devices):
    barrier = pltpu.get_barrier_semaphore()
    for device in devices:
        pl.semaphore_signal(barrier, inc=1, device_id=device, device_id_type=MESH)
    pl.semaphore_wait(barrier, len(devices))


class Messages:
    def __init__(self, send_sem, recv_sem):
        self.send_sem, self.recv_sem = send_sem, recv_sem
        self.index, self.sent = {}, []

    def copy(self, key, src, dst, device):
        slot = self.index.setdefault(key, len(self.index))
        return pltpu.make_async_remote_copy(
            src_ref=src, dst_ref=dst, send_sem=self.send_sem.at[slot], recv_sem=self.recv_sem.at[slot],
            device_id=device, device_id_type=MESH,
        )

    def send(self, key, src, dst, device):
        copy = self.copy(key, src, dst, device)
        copy.start()
        self.sent.append(copy)

    def arrive(self, key, dst, device):
        self.copy(key, dst, dst, device).wait_recv()

    def drain(self):
        for copy in self.sent:
            copy.wait_send()


def gather(messages, peers, place, own, group):
    half, z, core = place
    up, down, side, twin = peers

    def at(h, depth, c, start, size):
        position = h * 16 + lax.rem(depth + 2 * RING, RING) * 2 + c
        return group.at[pl.ds(position * SLAB + start, size)]

    low, high = (0, 4), (4, 4)
    shared, shared_low, shared_high = (2, 4), (2, 2), (4, 2)
    rest_low, rest_high = (0, 2), (6, 2)
    waiting = []

    def ring_send(way, step, mine, piece):
        dst = at(half if mine else 1 - half, z - way * (step - 1), core, *piece)
        src = own(*piece) if mine and step == 1 else dst
        messages.send(("ring", way, step, mine, piece), src, dst, up if way > 0 else down)

    def to_twin(key, here, owner, origin, piece):
        messages.send(("twin",) + key, here, here, twin)
        waiting.append((("twin",) + key, at(owner, origin, 1 - core, *piece)))

    def ring_arrive(way, step, mine, piece, last):
        origin, owner = z - way * step, half if mine else 1 - half
        here, key = at(owner, origin, core, *piece), ("ring", way, step, mine, piece)
        messages.arrive(key, here, up)
        if step < last:
            ring_send(way, step + 1, mine, piece)
        if mine:
            rest = rest_low if piece == low else rest_high
            part = at(half, origin, core, *rest)
            messages.send(("side", way, step, rest), part, part, side)
        to_twin(key, here, owner, origin, piece)

    def side_arrive(key, origin, piece):
        here = at(1 - half, origin, core, *piece)
        messages.arrive(key, here, side)
        to_twin(key, here, 1 - half, origin, piece)

    ring_send(1, 1, True, low)
    ring_send(-1, 1, True, high)
    messages.send(("side", 0, 0, shared), own(*shared), at(half, z, core, *shared), side)
    ring_send(1, 1, True, high)
    ring_send(-1, 1, True, low)
    for piece in (rest_low, rest_high):
        messages.send(("side", 0, 0, piece), own(*piece), at(half, z, core, *piece), side)
    messages.send(("twin", "own"), own(0, SLAB), at(half, z, core, 0, SLAB), twin)
    waiting.append((("twin", "own"), at(half, z, 1 - core, 0, SLAB)))
    yield 0

    for step in range(1, 5):
        ring_arrive(1, step, True, low, 4)
        yield step
        ring_arrive(-1, step, True, high, 4)
        yield step
        if step == 1:
            side_arrive(("side", 0, 0, shared), z, shared)
            for way, piece in ((1, shared_low), (-1, shared_high), (1, shared_high), (-1, shared_low)):
                ring_send(way, 1, False, piece)
            yield step
        if step < 4:
            ring_arrive(1, step, True, high, 3)
            yield step
            ring_arrive(-1, step, True, low, 3)
            yield step
        if step == 1:
            side_arrive(("side", 0, 0, rest_low), z, rest_low)
            side_arrive(("side", 0, 0, rest_high), z, rest_high)
            yield step
        ring_arrive(1, step, False, shared_low, 4)
        yield step
        ring_arrive(-1, step, False, shared_high, 4)
        yield step
        if step < 4:
            ring_arrive(1, step, False, shared_high, 3)
            yield step
            ring_arrive(-1, step, False, shared_low, 3)
            yield step
        side_arrive(("side", 1, step, rest_low), z - step, rest_low)
        side_arrive(("side", -1, step, rest_high), z + step, rest_high)
        yield step
        if step < 4:
            side_arrive(("side", 1, step, rest_high), z - step, rest_high)
            side_arrive(("side", -1, step, rest_low), z + step, rest_low)
            yield step
    for key, here in waiting:
        messages.arrive(key, here, twin)
    yield 5


def products(tables, values, group, running, sums, part):
    groups = values.shape[0] // STEPS // PIECES

    def body(g):
        total = running[...]
        for j in range(STEPS):
            s = g * STEPS + j
            product = jnp.dot(values[tables[0, s]], group[tables[1, s]], preferred_element_type=jnp.float32)
            total = product + total * tables[2, s].astype(jnp.float32)
            sums[s] = total.astype(sums.dtype)
        running[...] = total

    running[...] = jnp.zeros(running.shape, running.dtype)
    for piece in range(PIECES):
        pl.loop(piece * groups, (piece + 1) * groups)(body)
        yield

    @pl.loop(0, part.shape[0])
    def _(i):
        part[i] = sums[tables[3, i]] * tables[4, i].astype(jnp.float32).astype(sums.dtype)


def scatter(messages, peers, place, part, store_out, x_in, turn, total, relay, y_in):
    y_hi, x = place
    both = (1, -1)

    def chunk(far, way, start):
        band = 1 - y_hi if far else y_hi
        return (band * 4 + lax.rem(x + way + 4, 4)) * SLAB + start

    def x_send(kind, far, way, src):
        messages.send(("x", kind, far, way), src, x_in.at[kind, far, (way + 1) // 2], peers["x", way])

    def x_arrive(kind, far, way):
        here = x_in.at[kind, far, (way + 1) // 2]
        messages.arrive(("x", kind, far, way), here, peers["x", way])
        return here

    def through(way):
        return 0 if way > 0 else 4

    def first(far):
        for way in both:
            x_send(0, far, way, part.at[pl.ds(chunk(far, 2 * way, through(way)), 4)])
        for way in both:
            x_send(1, far, way, part.at[pl.ds(chunk(far, way, through(-way)), 4)])

    def second(far):
        for way in both:
            here, base, side = x_arrive(0, far, way), chunk(far, way, through(way)), (way + 1) // 2
            for t in range(4):
                both_parts = part[base + t].astype(jnp.float32) + here[t].astype(jnp.float32)
                turn[far, side, t] = both_parts.astype(turn.dtype)
            x_send(2, far, way, turn.at[far, side])

    def last(far, way, more, store):
        one, two, base = x_arrive(1, far, -way), x_arrive(2, far, way), chunk(far, 0, through(way))
        for t in range(4):
            value = part[base + t].astype(jnp.float32) + one[t].astype(jnp.float32) + two[t].astype(jnp.float32)
            if more is not None:
                value = value + more[t].astype(jnp.float32)
            store(t, value)

    first(1)
    yield
    second(1)
    first(0)
    yield
    for way in both:
        side = (way + 1) // 2

        def store_total(t, value):
            total[side, t] = value.astype(total.dtype)

        last(1, way, None, store_total)
        messages.send(("y", 0, way), total.at[side], relay.at[side], peers["y", way])
    yield
    second(0)
    yield
    for way in both:
        here = relay.at[(way + 1) // 2]
        messages.arrive(("y", 0, way), here, peers["y", way])
        messages.send(("y", 1, way), here, y_in.at[(way + 1) // 2], peers["y", way])
    yield
    for way in both:
        here = y_in.at[(way + 1) // 2]
        messages.arrive(("y", 1, way), here, peers["y", way])
        last(0, way, here, lambda t, value: store_out(through(way) + t, value))
    yield


def layer_kernel(tables, own, values_hbm, out, *scratch):
    values, sums = scratch[:2]
    groups, parts = scratch[2:4], scratch[4:6]
    buffers = (scratch[6:11], scratch[11:16])
    sems, values_sem, keep_sem, running = (scratch[16:18], scratch[18:20]), scratch[20], scratch[21], scratch[22]
    row, col = lax.axis_index("row"), lax.axis_index("col")
    half, z, core = row // 16, lax.rem(row // 2, RING), lax.rem(row, 2)
    y_hi, x = col // 4, lax.rem(col, 4)

    def ring_peer(h, depth, c):
        return {"row": h * 16 + lax.rem(depth + RING, RING) * 2 + c}

    def x_peer(way):
        return {"col": y_hi * 4 + lax.rem(x + way + 4, 4)}

    def y_peer(way):
        y = lax.rem(y_hi * 2 + half + way + 4, 4)
        return {"row": lax.rem(row, 16) + lax.rem(y, 2) * 16, "col": (y // 2) * 4 + x}

    ring = (ring_peer(half, z + 1, core), ring_peer(half, z - 1, core), ring_peer(1 - half, z, core), ring_peer(half, z, 1 - core))
    cross = {("x", 1): x_peer(1), ("x", -1): x_peer(-1), ("y", 1): y_peer(1), ("y", -1): y_peer(-1)}
    enter(ring + tuple(cross.values()))
    load = pltpu.make_async_copy(values_hbm, values, values_sem)

    gathers, scatters, keeps, talks = [], [], [], []
    for h in range(2):
        lanes = pl.ds(h * HALF, HALF)
        messages = Messages(*sems[h])
        talks.append(messages)

        def own_piece(start, size, lanes=lanes):
            return own.at[pl.ds(start, size), :, lanes]

        def store_out(t, value, lanes=lanes):
            out[t, :, lanes] = value.astype(out.dtype)

        gathers.append(gather(messages, ring, (half, z, core), own_piece, groups[h]))
        scatters.append(scatter(messages, cross, (y_hi, x), parts[h], store_out, *buffers[h]))
        keeps.append(pltpu.make_async_copy(own.at[:, :, lanes], groups[h].at[pl.ds(row * SLAB, SLAB)], keep_sem.at[h]))

    multiply = [products(tables, values, groups[h], running, sums, parts[h]) for h in range(2)]
    acts = {"g0": gathers[0], "g1": gathers[1], "s0": scatters[0], "s1": scatters[1], "m0": multiply[0], "m1": multiply[1]}
    next(gathers[0])
    for keep in keeps:
        keep.start()
    load.start()
    for name in ORDER:
        if name == "local":
            load.wait()
            for keep in keeps:
                keep.wait()
        else:
            next(acts[name], None)
    for gen in acts.values():
        for _ in gen:
            pass
    for messages in talks:
        messages.drain()
        assert len(messages.index) == COPIES


def spread(*lists):
    tagged = []
    for n, items in enumerate(lists):
        tagged += [((i + 0.5) / len(items), n, item) for i, item in enumerate(items)]
    return [item for _, _, item in sorted(tagged)]


ORDER = (
    ["g0"] * 32 + ["g1"] + ["g0"] * 6 + ["local"]
    + spread(["m0"] * (PIECES + 1), ["g1"] * 12) + ["s0"]
    + ["g1"] * 10 + ["s0"]
    + ["g1"] * 5 + ["s0"] + ["g1"] * 5 + ["s0"]
    + ["g1"] * 5 + ["s0"] + ["g1"]
    + ["m1"] * (PIECES + 1) + ["s1"] + ["s0"] + ["s1"] * 5
)


def layer(tables, own, values):
    slab, side, width = own.shape
    tiles = values.shape[0]
    bf16 = own.dtype
    piece = (4, side, HALF)
    vmem = pl.BlockSpec(memory_space=pltpu.VMEM)
    sums = pltpu.VMEM((tiles, side, HALF), bf16)
    group = pltpu.VMEM((4 * RING * slab, side, HALF), bf16)
    part = pltpu.VMEM((8 * slab, side, HALF), bf16)
    buffers = [
        pltpu.VMEM((3, 2, 2) + piece, bf16),
        pltpu.VMEM((2, 2) + piece, bf16),
        pltpu.VMEM((2,) + piece, bf16),
        pltpu.VMEM((2,) + piece, bf16),
        pltpu.VMEM((2,) + piece, bf16),
    ]
    sems = [pltpu.SemaphoreType.DMA((COPIES,)), pltpu.SemaphoreType.DMA((COPIES,))]
    return pl.pallas_call(
        layer_kernel,
        out_shape=jax.ShapeDtypeStruct((slab, side, width), bf16),
        in_specs=[pl.BlockSpec(memory_space=pltpu.SMEM), vmem, pl.BlockSpec(memory_space=pl.ANY)],
        out_specs=vmem,
        scratch_shapes=[pltpu.VMEM(values.shape, bf16), sums, group, group, part, part]
        + buffers + buffers + sems + sems + [pltpu.SemaphoreType.DMA, pltpu.SemaphoreType.DMA((2,)), pltpu.VMEM((side, HALF), jnp.float32)],
        compiler_params=pltpu.CompilerParams(collective_id=0, has_side_effects=True, vmem_limit_bytes=60 * 1024 * 1024),
        name="layer",
    )(tables, own, values)


def local(features, tile_values, tile_rows, tile_cols, tile_count, weight):
    slab_rows, width = features.shape
    tiles, side = tile_values.shape[2:4]
    tables = plan(tile_count.reshape(1), tile_rows.reshape(1, tiles), tile_cols.reshape(1, tiles))
    summed = layer(tables, features.reshape(-1, side, width), tile_values.reshape(tiles, side, side))
    return jnp.dot(summed.reshape(slab_rows, width), weight, preferred_element_type=jnp.float32).astype(jnp.bfloat16)


def solution(mesh):
    return jax.shard_map(
        local,
        mesh=mesh,
        in_specs=(
            P(("row", "col"), None),
            P("row", "col", None, None, None),
            P("row", "col", None),
            P("row", "col", None),
            P("row", "col"),
            P(),
        ),
        out_specs=P(("row", "col"), None),
        check_vma=False,
    )
```

time: 393 us -> 120 us (0.31)
  waiting for transfers between devices: 222 us -> 0 us
  Pallas kernels: 0 us -> 117 us
  other arithmetic: 86.8 us -> 0 us
  local copies, waits for them, and re-layouts: 38.8 us -> 0.01 us
  matrix products: 31.6 us -> 2.13 us
  between operations: 13.4 us -> 0.71 us
    pallas_call x0 -> x2, Pallas kernels: none -> 117 us  [the longest x1 115 us: layer(): pl.pallas_call(layer_kernel, out_shape=jax.ShapeDtypeStruct((slab, side,...]
    psum x1 -> x0, waiting for transfers between devices: 115 us -> none  [local(): lax.psum(partial_value.astype(jnp.bfloat16), 'col').astype(jnp.float32)]
    all_gather x1 -> x0, waiting for transfers between devices: 106 us -> none  [local(): group = lax.all_gather(features, 'row', axis=0, tiled=True)]
    scatter-add x4 -> x0, other arithmetic: 77.7 us -> none  [accumulate(): return carry.at[targets].add(products)]
    gather x4 -> x0, local copies, waits for them, and re-layouts: 34.5 us -> none  [accumulate(): inputs = jnp.take(col_tiles, picks, axis=0)]
    dot_general x5 -> x1, matrix products: 31.6 us -> 2.13 us  [local(): jnp.dot(summed.reshape(slab_rows, width), weight, preferred_element_type=...]
    convert_element_type x1 -> x0, other arithmetic: 5.93 us -> none  [local(): carry.reshape(row_tiles * side, width).astype(jnp.bfloat16)]
    broadcast_in_dim x1 -> x0, local copies, waits for them, and re-layouts: 4.24 us -> none  [local(): jnp.zeros((row_tiles, side, width), jnp.float32)]
  transfers between devices with their start and end apart: 2 -> 0, of which waited for: 2 -> 0; matrix products, arithmetic and copies ran while one was open for 0% -> 0% of each run, Pallas kernels for 0% -> 0%
where the time goes in v3:
time: 120 us
  Pallas kernels  117 us (98%)
  matrix products  2.13 us (2%)
    pallas_call x1, Pallas kernels, layer(): pl.pallas_call(layer_kernel, out_shape=jax.ShapeDtypeStruct((slab, side,...  115 us

profile of v3, /device:TPU:1, one launch (start us, length us, event | category | flops | bytes accessed | tf_op | source)
XLA Modules:
  0.0 119.7 jit_solution(747262838118456421)
XLA Ops:
  0.0 0.0 copy-start
  0.7 1.6 %plan.1.tables = s32[8,256]{1,0:T(8,128)} custom-call(s32[1]{0:T(128)} %bitcast.8.count, s32[1,256]{1,0:T(1,128)} %bitcast.12, s32[1,256]{1,0:T(1,128)} %bitcast.13), custom_call_target="tpu_custom_call" | custom-call | tf_op jit(solution)/shard_map/plan/pallas_call | solution.py:50
  2.3 115.3 %layer.1 = bf16[8,128,256]{2,1,0:T(8,128)(2,1)} custom-call(s32[8,256]{1,0:T(8,128)} %plan.1.tables, bf16[8,128,256]{2,1,0:T(8,128)(2,1)} %bitcast.11, bf16[256,128,128]{2,1,0:T(8,128)(2,1)} %bitcast.9), custom_call_target="tpu_custom_call" | custom-call | tf_op jit(solution)/shard_map/layer/pallas_call | solution.py:367
  117.6 0.0 copy-done
  117.6 2.1 %convolution_convert_fusion = bf16[1024,256]{1,0:T(8,128)(2,1)} fusion(bf16[1024,256]{1,0:T(8,128)(2,1)} %bitcast.10, bf16[256,256]{1,0:T(8,128)(2,1)S(1)} %copy-done), kind=kOutput, calls=%fused_computation | convolution fusion | flops 134479872 | bytes 1179648 | tf_op jit(solution)/shard_map/dot_general | solution.py:384
Async XLA Ops:
  0.0 117.6 %copy-start = (bf16[256,256]{1,0:T(8,128)(2,1)S(1)}, bf16[256,256]{1,0:T(8,128)(2,1)}, u32[]{:S(2)}) copy-start(bf16[256,256]{1,0:T(8,128)(2,1)} %param.11) | copy-start | bytes 393220
